TPU v7x, 32 devices: a whole 2x2x4 slice. The times are simulated.
32 devices in a mesh: dp: 8 (over y, x, core), expert: 4 (over z).
Axes of the slice: x: 2, y: 2, z: 4, core: 2. Of those that a mesh axis runs over, the one named last changes fastest.
Arguments:
- tokens: bfloat16 [4096, 2048], P(('dp', 'expert')), may hold values from -6 to 6
- w_qkv: bfloat16 [3, 2048, 2048], P(None, 'dp', 'expert'), may hold values from -0.125 to 0.125
- w_out: bfloat16 [2048, 2048], P('expert', 'dp'), may hold values from -0.5 to 0.5
- attention_norm_gain: bfloat16 [2048], P('dp'), may hold values from 0.5 to 1.5
- gain_ffn: bfloat16 [2048], P('dp'), may hold values from 0.5 to 1.5
- w_router: bfloat16 [2048, 4], P('dp'), may hold values from -0.09375 to 0.09375
- w_gate_up: bfloat16 [4, 2048, 11264], P('expert', 'dp'), may hold values from -0.125 to 0.125
- w_down: bfloat16 [4, 5632, 2048], P('expert', 'dp'), may hold values from -0.15625 to 0.15625
- lengths: int32 [8], P('dp'), may hold values from 128 to 512, as said below
- routes: int32 [4096, 2], P(('dp', 'expert')), may hold values from 0 to 3, all different within a row
- order: int32 [4096], P(('dp', 'expert')), may hold values from 0 to 127, as said below
- cotangent: bfloat16 [4096, 2048], P(('dp', 'expert')), may hold values from -6 to 6
Outputs:
- output: bfloat16 [4096, 2048], P(('dp', 'expert'))
- grad_tokens: bfloat16 [4096, 2048], P(('dp', 'expert'))
- grad_qkv: float32 [3, 2048, 2048], P(None, 'dp', 'expert')
- grad_out: float32 [2048, 2048], P('expert', 'dp')
- grad_gain_attn: float32 [2048], P('dp')
- grad_gain_ffn: float32 [2048], P('dp')
- grad_router: float32 [2048, 4], P('dp')
- grad_gate_up: float32 [4, 2048, 11264], P('expert', 'dp')
- grad_down: float32 [4, 5632, 2048], P('expert', 'dp')
Inputs may be any that keep to these rules, and one draw needn't show every extreme that they name: `lengths`: one sequence of every draw has exactly 512 live tokens. `routes`: each token slot names 2 different experts, and every expert is named somewhere. `order`: each aligned block of 128 entries holds every number of 0 to 127 once.
All inputs are finite; a program needn't handle non-finite values.
Results may differ from a plain program's by a relative error of at most 0.023.
Values may be sent and summed in bfloat16 or wider, within the bound.
A program may use at most 384 MiB of HBM per device.

v0:
```python
import jax
import jax.numpy as jnp
from jax import lax
from jax.sharding import PartitionSpec as P

HEAD_DIM = 128
FF = 5632
NORM_EPSILON = 1e-05
NEGATIVE = -1e30
THETA = 10000.0
HIGH = lax.Precision.HIGHEST


def rotary_tables(length_total, head_size):
    position = jnp.arange(length_total, dtype=jnp.float32)
    frequency = THETA ** (-(jnp.arange(head_size // 2, dtype=jnp.float32) * 2.0 / head_size))
    angles = position[:, None] * frequency[None, :]
    return (jnp.cos(angles)[:, None, :], jnp.sin(angles)[:, None, :])


def rotate(values, cosine, sine):
    half_size = values.shape[-1] // 2
    first = values[..., :half_size]
    second = values[..., half_size:]
    return jnp.concatenate(
        [first * cosine - second * sine, second * cosine + first * sine], axis=-1
    )


def rotate_back(grad_rows, cosine, sine):
    half_size = grad_rows.shape[-1] // 2
    first = grad_rows[..., :half_size]
    second = grad_rows[..., half_size:]
    return jnp.concatenate(
        [first * cosine + second * sine, second * cosine - first * sine], axis=-1
    )


def slot_table(routes, order, valid, capacity):
    row_count = routes.shape[0]
    top_count = routes.shape[1]
    pair_rank = order[:, None] + row_count * jnp.arange(top_count, dtype=jnp.int32)[None, :]
    flat_rank = pair_rank.reshape(-1)
    flat_expert = routes.reshape(-1)
    flat_valid = jnp.broadcast_to(valid[:, None], routes.shape).reshape(-1)
    earlier = (
        (flat_rank[None, :] < flat_rank[:, None])
        & (flat_expert[None, :] == flat_expert[:, None])
        & flat_valid[None, :]
    )
    slot_index = jnp.sum(earlier.astype(jnp.int32), axis=1).reshape(row_count, top_count)
    kept_pair = valid[:, None] & (slot_index < capacity)
    target = routes * capacity + jnp.minimum(slot_index, capacity - 1)
    return (target, kept_pair)


def masked_scores(query, key_rows, allowed):
    scale = query.shape[-1] ** (-0.5)
    raw = jnp.einsum("qhd,khd->hqk", query, key_rows, preferred_element_type=jnp.float32) * scale
    return jnp.where(allowed[None], raw, NEGATIVE)


def contract_first(left, right):
    return lax.dot_general(
        left, right, (((0,), (0,)), ((), ())), preferred_element_type=jnp.float32
    )


def contract_last(left, right):
    return lax.dot_general(
        left, right, (((1,), (1,)), ((), ())), preferred_element_type=jnp.float32
    )


def normalize(rows):
    inverse = lax.rsqrt(jnp.mean(rows * rows, axis=-1, keepdims=True) + NORM_EPSILON)
    return (rows * inverse, inverse)


def exchange_experts(blocks):
    return lax.all_to_all(blocks, "expert", split_axis=0, concat_axis=0, tiled=True)


def by_hidden(w_gate_up):
    parts = lax.axis_size("dp")
    rows = w_gate_up.shape[1]
    ff_part = w_gate_up.shape[2] // 2 // parts
    pieces = w_gate_up[0].reshape(rows, 2, parts, ff_part).transpose(2, 0, 1, 3)
    pieces = pieces.reshape(parts, rows, 2 * ff_part)
    got = lax.all_to_all(pieces, "dp", split_axis=0, concat_axis=0, tiled=True)
    return got.reshape(parts * rows, 2 * ff_part)


def by_rows(grad):
    parts = lax.axis_size("dp")
    rows = grad.shape[0] // parts
    ff_part = grad.shape[1] // 2
    pieces = grad.astype(jnp.bfloat16).reshape(parts, rows, 2 * ff_part)
    got = lax.all_to_all(pieces, "dp", split_axis=0, concat_axis=0, tiled=True)
    got = got.reshape(parts, rows, 2, ff_part).transpose(1, 2, 0, 3)
    return got.reshape(1, rows, 2 * parts * ff_part).astype(jnp.float32)


def expert_step(gate_up_w, down_w, rows, d_rows_out):
    ff = down_w.shape[0]
    gate_up = jnp.dot(rows, gate_up_w, preferred_element_type=jnp.float32)
    gate = gate_up[:, :ff]
    upward = gate_up[:, ff:]
    sigmoid = jax.nn.sigmoid(gate)
    activated = (gate * sigmoid * upward).astype(jnp.bfloat16)
    out = jnp.dot(activated, down_w, preferred_element_type=jnp.float32).astype(jnp.bfloat16)
    d_activated = contract_last(d_rows_out, down_w)
    grad_down = contract_first(activated, d_rows_out)
    d_gate = d_activated * upward * sigmoid * (1.0 + gate * (1.0 - sigmoid))
    d_up = d_activated * gate * sigmoid
    d_gate_up = jnp.concatenate([d_gate, d_up], axis=1).astype(jnp.bfloat16)
    d_rows = contract_last(d_gate_up, gate_up_w).astype(jnp.bfloat16)
    grad_gate_up = contract_first(rows, d_gate_up)
    return (out, d_rows, grad_gate_up, grad_down)


def experts_split_hidden(w_gate_up, w_down, rows, d_rows_out):
    gate_up_w = by_hidden(w_gate_up)
    all_rows = lax.all_gather(rows, "dp", axis=0, tiled=True)
    all_d_out = lax.all_gather(d_rows_out, "dp", axis=0, tiled=True)
    out, d_rows, grad_gate_up, grad_down = expert_step(gate_up_w, w_down[0], all_rows, all_d_out)
    out = lax.psum_scatter(out, "dp", scatter_dimension=0, tiled=True)
    d_rows = lax.psum_scatter(d_rows, "dp", scatter_dimension=0, tiled=True)
    return (out, d_rows, by_rows(grad_gate_up), grad_down[None])


def experts_gather_weights(w_gate_up, w_down, rows, d_rows_out):
    gate_up_w = lax.all_gather(w_gate_up, "dp", axis=1, tiled=True)[0]
    down_w = lax.all_gather(w_down, "dp", axis=1, tiled=True)[0]
    out, d_rows, grad_gate_up, grad_down = expert_step(gate_up_w, down_w, rows, d_rows_out)
    grad_gate_up = lax.psum_scatter(
        grad_gate_up.astype(jnp.bfloat16), "dp", scatter_dimension=0, tiled=True
    )
    grad_down = lax.psum_scatter(
        grad_down.astype(jnp.bfloat16), "dp", scatter_dimension=0, tiled=True
    )
    return (
        out,
        d_rows,
        grad_gate_up.astype(jnp.float32)[None],
        grad_down.astype(jnp.float32)[None],
    )


def on_device(
    tokens,
    w_qkv,
    w_out,
    attention_norm_gain,
    gain_ffn,
    w_router,
    w_gate_up,
    w_down,
    lengths,
    routes,
    order,
    cotangent,
):
    group_size = lax.axis_size("expert")
    dp_size = lax.axis_size("dp")
    tok_dev = tokens.shape[0]
    seq_len = tok_dev * group_size
    width = tokens.shape[1]
    top_count = routes.shape[1]
    capacity = tok_dev * top_count // group_size
    slots = group_size * capacity
    head_size = HEAD_DIM
    local_width = w_qkv.shape[2]
    heads_local = local_width // head_size
    tokens_all = lax.all_gather(tokens, "expert", axis=0, tiled=True)
    small = jnp.concatenate([attention_norm_gain[:, None], gain_ffn[:, None], w_router], axis=1)
    small_full = lax.all_gather(small, "dp", axis=0, tiled=True)
    qkv_full = lax.all_gather(w_qkv, "dp", axis=1, tiled=True)
    out_full = lax.all_gather(w_out, "dp", axis=1, tiled=True)
    first_norm_gain = small_full[:, 0].astype(jnp.float32)
    gain_two = small_full[:, 1].astype(jnp.float32)
    router_full = small_full[:, 2:]
    own_start = lax.axis_index("expert") * tok_dev
    own_position = own_start + jnp.arange(tok_dev, dtype=jnp.int32)
    live_own = own_position < lengths[0]
    live_rows = live_own.astype(jnp.float32)[:, None]
    target, kept_pair = slot_table(routes, order, live_own, capacity)
    slot_ids = jnp.arange(slots, dtype=jnp.int32)
    pair_hits = (slot_ids[:, None, None] == target[None]) & kept_pair[None]
    select = jnp.sum(pair_hits.astype(jnp.float32), axis=2).astype(jnp.bfloat16)
    inputs_float = tokens.astype(jnp.float32)
    input_normalized_hat, first_inverse_rms = normalize(inputs_float)
    hat_all, _ = normalize(tokens_all.astype(jnp.float32))
    whole = (hat_all * first_norm_gain).astype(jnp.bfloat16)
    cosine, sine = rotary_tables(seq_len, head_size)
    projected = jnp.einsum("td,cde->cte", whole, qkv_full, preferred_element_type=jnp.float32)
    query = rotate(projected[0].reshape(seq_len, heads_local, head_size), cosine, sine).astype(
        jnp.bfloat16
    )
    key_rows = rotate(projected[1].reshape(seq_len, heads_local, head_size), cosine, sine).astype(
        jnp.bfloat16
    )
    value = projected[2].astype(jnp.bfloat16).reshape(seq_len, heads_local, head_size)
    position = jnp.arange(seq_len, dtype=jnp.int32)
    live_all = position < lengths[0]
    allowed = (position[None, :] <= position[:, None]) & live_all[None, :]
    scores = masked_scores(query, key_rows, allowed)
    top_score = jnp.max(scores, axis=-1, keepdims=True)
    exponent = jnp.exp(scores - top_score)
    row_total = jnp.sum(exponent, axis=-1, keepdims=True)
    probs = exponent / row_total
    log_total = top_score + jnp.log(row_total)
    probs_low = probs.astype(jnp.bfloat16)
    attended = jnp.einsum("hqk,khd->qhd", probs_low, value, preferred_element_type=jnp.float32)
    attended = attended.reshape(seq_len, local_width).astype(jnp.bfloat16)
    attn_part = jnp.dot(attended, out_full, preferred_element_type=jnp.float32)
    attn_own = lax.psum_scatter(
        attn_part.astype(jnp.bfloat16), "expert", scatter_dimension=0, tiled=True
    ).astype(jnp.float32)
    resid = inputs_float + attn_own
    hhat, inverse_two = normalize(resid)
    hidden_in = (hhat * gain_two).astype(jnp.bfloat16)
    sent = jnp.dot(select, hidden_in, preferred_element_type=jnp.float32).astype(jnp.bfloat16)
    dispatched = exchange_experts(sent.reshape(group_size, capacity, width)).reshape(slots, width)
    logits = jnp.dot(hidden_in, router_full, preferred_element_type=jnp.float32)
    chosen = jnp.take_along_axis(logits, routes, axis=1)
    gates = jax.nn.softmax(chosen, axis=1)
    d_out = live_rows * cotangent.astype(jnp.float32)
    d_back = jnp.zeros((slots, width), jnp.float32)
    for index in range(top_count):
        weighted = (gates[:, index : index + 1] * d_out).astype(jnp.bfloat16)
        d_back = d_back + jnp.dot(
            pair_hits[:, :, index].astype(jnp.bfloat16),
            weighted,
            preferred_element_type=jnp.float32,
        )
    d_back = d_back.astype(jnp.bfloat16)
    d_out_rows = exchange_experts(d_back.reshape(group_size, capacity, width)).reshape(slots, width)
    split_cost = 4 * dp_size * slots * width + 2 * 2 * FF * width // dp_size
    gather_cost = 2 * 3 * FF * width
    experts = experts_split_hidden if split_cost < gather_cost else experts_gather_weights
    expert_out, d_rows, grad_gate_up, grad_down = experts(w_gate_up, w_down, dispatched, d_out_rows)
    d_sent = exchange_experts(d_rows.reshape(group_size, capacity, width)).reshape(slots, width)
    returned = exchange_experts(expert_out.reshape(group_size, capacity, width)).reshape(
        slots, width
    )
    moe = jnp.zeros_like(resid)
    d_gates_list = []
    for index in range(top_count):
        one_hot = pair_hits[:, :, index].astype(jnp.bfloat16)
        picked = contract_first(one_hot, returned)
        d_gates_list.append(jnp.sum(d_out * picked, axis=-1))
        moe = moe + gates[:, index : index + 1] * picked
    output = (live_rows * (resid + moe)).astype(jnp.bfloat16)
    d_gates = jnp.stack(d_gates_list, axis=1)
    d_hidden = contract_first(select, d_sent)
    d_chosen = gates * (d_gates - jnp.sum(gates * d_gates, axis=1, keepdims=True))
    expert_ids = jnp.arange(group_size, dtype=jnp.int32)
    route_hits = (routes[:, :, None] == expert_ids[None, None, :]).astype(jnp.float32)
    d_logits = jnp.sum(route_hits * d_chosen[:, :, None], axis=1)
    router_f = router_full.astype(jnp.float32)
    d_hidden = d_hidden + jnp.dot(
        d_logits, router_f.T, precision=HIGH, preferred_element_type=jnp.float32
    )
    router_part = jnp.dot(
        hidden_in.astype(jnp.float32).T,
        d_logits,
        precision=HIGH,
        preferred_element_type=jnp.float32,
    )
    gain_two_part = jnp.sum(d_hidden * hhat, axis=0)
    scaled_two = d_hidden * gain_two
    d_resid = d_out + inverse_two * (
        scaled_two - hhat * jnp.mean(scaled_two * hhat, axis=-1, keepdims=True)
    )
    d_attn = d_resid.astype(jnp.bfloat16)
    whole_grad = lax.all_gather(d_attn, "expert", axis=0, tiled=True)
    d_attended = contract_last(whole_grad, out_full).astype(jnp.bfloat16)
    out_part = contract_first(attended, whole_grad)
    grad_out = lax.psum_scatter(
        out_part.astype(jnp.bfloat16), "dp", scatter_dimension=1, tiled=True
    ).astype(jnp.float32)
    d_heads = d_attended.reshape(seq_len, heads_local, head_size)
    probs = jnp.exp(masked_scores(query, key_rows, allowed) - log_total)
    probs_low = probs.astype(jnp.bfloat16)
    d_value = jnp.einsum(
        "hqk,qhd->khd", probs_low, d_heads, preferred_element_type=jnp.float32
    ).astype(jnp.bfloat16)
    d_probs = jnp.einsum("qhd,khd->hqk", d_heads, value, preferred_element_type=jnp.float32)
    row_delta = jnp.sum(probs * d_probs, axis=-1, keepdims=True)
    d_scores = (probs * (d_probs - row_delta)).astype(jnp.bfloat16)
    scale = head_size ** (-0.5)
    d_query = (
        jnp.einsum("hqk,khd->qhd", d_scores, key_rows, preferred_element_type=jnp.float32) * scale
    )
    d_key = jnp.einsum("hqk,qhd->khd", d_scores, query, preferred_element_type=jnp.float32) * scale
    d_query_pre = (
        rotate_back(d_query, cosine, sine).reshape(seq_len, local_width).astype(jnp.bfloat16)
    )
    d_key_pre = rotate_back(d_key, cosine, sine).reshape(seq_len, local_width).astype(jnp.bfloat16)
    d_projected = jnp.stack([d_query_pre, d_key_pre, d_value.reshape(seq_len, local_width)])
    d_normed_part = jnp.einsum(
        "cte,cde->td", d_projected, qkv_full, preferred_element_type=jnp.float32
    )
    grad_normalized = lax.psum_scatter(
        d_normed_part.astype(jnp.bfloat16), "expert", scatter_dimension=0, tiled=True
    ).astype(jnp.float32)
    qkv_part = jnp.einsum("td,cte->cde", whole, d_projected, preferred_element_type=jnp.float32)
    grad_qkv = lax.psum_scatter(
        qkv_part.astype(jnp.bfloat16), "dp", scatter_dimension=1, tiled=True
    ).astype(jnp.float32)
    first_gain_part = jnp.sum(d_normed_part * hat_all, axis=0)
    first_scaled_input = grad_normalized * first_norm_gain
    grad_tokens = d_resid + first_inverse_rms * (
        first_scaled_input
        - input_normalized_hat
        * jnp.mean(first_scaled_input * input_normalized_hat, axis=-1, keepdims=True)
    )
    small_part = jnp.concatenate(
        [first_gain_part[None], gain_two_part[None], router_part.T], axis=0
    )
    small_sum = lax.psum(small_part, ("dp", "expert"))
    own_rows = width // dp_size
    small_own = lax.dynamic_slice_in_dim(
        small_sum, lax.axis_index("dp") * own_rows, own_rows, axis=1
    )
    return (
        output,
        grad_tokens.astype(jnp.bfloat16),
        grad_qkv,
        grad_out,
        small_own[0],
        small_own[1],
        small_own[2:].T,
        grad_gate_up,
        grad_down,
    )


def solution(mesh):
    placed = (
        P(("dp", "expert"), None),
        P(None, "dp", "expert"),
        P("expert", "dp"),
        P("dp"),
        P("dp"),
        P("dp", None),
        P("expert", "dp", None),
        P("expert", "dp", None),
        P("dp"),
        P(("dp", "expert"), None),
        P(("dp", "expert")),
        P(("dp", "expert"), None),
    )
    return jax.shard_map(
        on_device,
        mesh=mesh,
        in_specs=placed,
        out_specs=(
            P(("dp", "expert"), None),
            P(("dp", "expert"), None),
            P(None, "dp", "expert"),
            P("expert", "dp"),
            P("dp"),
            P("dp"),
            P("dp", None),
            P("expert", "dp", None),
            P("expert", "dp", None),
        ),
        check_vma=False,
    )
```

profile of v0, /device:TPU:10, one launch (start us, length us, event | category | flops | bytes accessed | tf_op | source)
XLA Modules:
  0.0 981.0 jit_solution(3513390332413267402)
XLA Ops:
  8.0 2.4 copy.213
  13.8 9.1 all_gather.22
  23.8 1.7 fusion.41
  25.5 29.6 %all-gather.7.cloned.1.call-done = bf16[512,2048]{1,0:T(8,128)(2,1)} async-done(((bf16[128,2048]{1,0:T(8,128)(2,1)}), bf16[512,2048]{1,0:T(8,128)(2,1)}) %all-gather.7.cloned.1.call-update) | async-done | bytes 2097168 | tf_op jit(solution)/shard_map/all_gather | solution.py:175
  55.1 2.1 fusion.4
  57.2 47.4 %all-gather.9.cloned.1.call-done = bf16[3,2048,512]{1,2,0:T(8,128)(2,1)} async-done(((bf16[3,256,512]{1,2,0:T(8,128)(2,1)}), bf16[3,2048,512]{1,2,0:T(8,128)(2,1)}) %all-gather.9.cloned.1.call-update) | async-done | bytes 6291472 | tf_op jit(solution)/shard_map/all_gather | solution.py:178
  104.6 6.4 convolution_bitcast_fusion.1
  113.9 2.4 copy.260
  116.2 2.2 fusion.66
  118.5 2.4 copy.262
  120.8 1.3 copy.259
  122.2 2.4 copy.261
  124.5 3.3 subtract_convert_fusion.3
  127.8 1.4 fusion.68
  129.9 1.4 copy-done.2
  131.3 1.7 fusion.21
  133.0 1.7 all-gather.11.cloned.1.call-done
  134.7 4.4 convolution_convert_fusion.4
  141.3 39.6 %reduce-scatter.7.cloned.1.call-done = bf16[128,2048]{1,0:T(8,128)(2,1)} async-done(((bf16[512,2048]{1,0:T(8,128)(2,1)}), bf16[128,2048]{1,0:T(8,128)(2,1)}) %reduce-scatter.7.cloned.1.call-update) | async-done | bytes 524304 | tf_op jit(solution)/shard_map/reduce_scatter | solution.py:217
  180.9 1.3 multiply_reduce_fusion.5
  184.7 30.0 %all_to_all.30 = bf16[4,64,2048]{2,1,0:T(8,128)(2,1)} all-to-all(bf16[4,64,2048]{2,1,0:T(8,128)(2,1)S(1)} %bitcast.127), channel_id=1, replica_groups=mesh['dp'=8,'expert'=4] {'expert'}, dimensions={0} | all-to-all | bytes 2097152 | tf_op jit(solution)/shard_map/all_to_all | solution.py:81
  215.0 8.4 copy.224
  223.4 3.4 copy.225
  226.8 94.9 %all_to_all.31 = bf16[8,256,1408]{1,2,0:T(8,128)(2,1)} all-to-all(bf16[8,256,1408]{1,2,0:T(8,128)(2,1)S(1)} %bitcast.119), channel_id=1, replica_groups=mesh['dp'=8,'expert'=4] {'dp'}, dimensions={0} | all-to-all | bytes 11534336 | tf_op jit(solution)/shard_map/all_to_all | solution.py:90
  321.7 8.2 copy.226
  329.9 18.8 %fusion.69 = f32[2048,1408]{0,1:T(8,128)} fusion(bf16[2048,2048]{1,0:T(8,128)(2,1)} %all-gather.13.cloned.1.call-done, bf16[2048,1408]{1,0:T(8,128)(2,1)} %bitcast.121), kind=kOutput, calls=%fused_computation.161 | convolution fusion | flops 11811160064 | bytes 25690112 | tf_op jit(solution)/shard_map/dot_general | solution.py:106
  348.7 5.2 multiply_convert_fusion.2
  354.0 1.7 copy-done.22
  355.7 9.1 convolution_convert_fusion.1
  364.7 71.4 %reduce-scatter.9.cloned.1.call-done = bf16[256,2048]{1,0:T(8,128)(2,1)} async-done(((bf16[2048,2048]{1,0:T(8,128)(2,1)}), bf16[256,2048]{1,0:T(8,128)(2,1)}) %reduce-scatter.9.cloned.1.call-update) | async-done | bytes 1048592 | tf_op jit(solution)/shard_map/reduce_scatter | solution.py:127
  436.1 5.1 all-to-all-start.2
  443.9 2.4 gather_fusion
  447.1 1.5 copy.220
  449.8 13.9 %all-to-all-done.2 = bf16[4,64,2048]{2,1,0:T(8,128)(2,1)} async-done(((bf16[4,64,2048]{2,1,0:T(8,128)(2,1)}), bf16[4,64,2048]{2,1,0:T(8,128)(2,1)}, u32[]{:S(2)}, u32[]{:S(2)}) %all-to-all-start.2) | async-done | bytes 1048608 | tf_op jit(solution)/shard_map/all_to_all | solution.py:81
  463.7 1.6 fusion.44
  466.3 2.8 multiply_reduce_fusion.4
  471.4 29.9 %all_to_all.32 = bf16[4,64,2048]{2,1,0:T(8,128)(2,1)} all-to-all(bf16[4,64,2048]{2,1,0:T(8,128)(2,1)S(1)} %bitcast.130), channel_id=1, replica_groups=mesh['dp'=8,'expert'=4] {'expert'}, dimensions={0} | all-to-all | bytes 2097152 | tf_op jit(solution)/shard_map/all_to_all | solution.py:81
  501.4 54.0 %all-gather.15.cloned.1.call-done = bf16[2048,2048]{1,0:T(8,128)(2,1)} async-done(((bf16[256,2048]{1,0:T(8,128)(2,1)}), bf16[2048,2048]{1,0:T(8,128)(2,1)}) %all-gather.15.cloned.1.call-update) | async-done | bytes 8388624 | tf_op jit(solution)/shard_map/all_gather | solution.py:125
  555.4 13.1 %multiply_convert_fusion.1 = (bf16[2048,704]{0,1:T(8,128)(2,1)S(1)}, bf16[2048,704]{0,1:T(8,128)(2,1)S(1)}) fusion(f32[2048,1408]{0,1:T(8,128)} %fusion.69, bf16[2048,2048]{1,0:T(8,128)(2,1)} %all-gather.15.cloned.1.call-done, bf16[1,704,2048]{2,1,0:T(8,128)(2,1)S(1)} %copy-done), kind=kOutput, calls=%fused_computation.8 | convolution fusion | flops 5924323328 | bytes 28573696 | tf_op jit(solution)/shard_map/dot_general | solution.py:70
  568.5 1.5 copy-done.62
  570.9 17.7 %convolution_convert_fusion = bf16[2048,2048]{1,0:T(8,128)(2,1)} fusion(bf16[2048,1408]{1,0:T(8,128)(2,1)} %bitcast.122, bf16[2048,704]{0,1:T(8,128)(2,1)S(1)} %get-tuple-element.75, bf16[2048,704]{0,1:T(8,128)(2,1)S(1)} %get-tuple-element.74), kind=kOutput, calls=%fused_computation.2 | convolution fusion | flops 11826888704 | bytes 19922944 | tf_op jit(solution)/shard_map/dot_general | solution.py:70
  588.7 71.3 %reduce-scatter.11.cloned.1.call-done = bf16[256,2048]{1,0:T(8,128)(2,1)} async-done(((bf16[2048,2048]{1,0:T(8,128)(2,1)}), bf16[256,2048]{1,0:T(8,128)(2,1)}) %reduce-scatter.11.cloned.1.call-update) | async-done | bytes 1048592 | tf_op jit(solution)/shard_map/reduce_scatter | solution.py:128
  660.0 5.1 all-to-all-start.4
  665.4 22.2 %all-to-all-done.4 = bf16[4,64,2048]{2,1,0:T(8,128)(2,1)S(1)} async-done(((bf16[4,64,2048]{2,1,0:T(8,128)(2,1)}), bf16[4,64,2048]{2,1,0:T(8,128)(2,1)S(1)}, u32[]{:S(2)}, u32[]{:S(2)}) %all-to-all-start.4) | async-done | bytes 1048608 | tf_op jit(solution)/shard_map/all_to_all | solution.py:81
  690.4 45.3 %all-gather.17.cloned.1.call-done = bf16[512,2048]{1,0:T(8,128)(2,1)} async-done(((bf16[128,2048]{1,0:T(8,128)(2,1)}), bf16[512,2048]{1,0:T(8,128)(2,1)}) %all-gather.17.cloned.1.call-update) | async-done | bytes 2097168 | tf_op jit(solution)/shard_map/all_gather | solution.py:277
  735.7 4.2 convolution_convert_fusion.3
  740.0 3.7 convolution_convert_fusion.6
  745.6 3.4 multiply_reduce_fusion
  756.7 9.5 bitcast_convert_fusion
  766.5 6.9 convert_bitcast_fusion.1
  773.5 19.1 %convolution_convert_fusion.2 = bf16[2048,1408]{1,0:T(8,128)(2,1)} fusion(bf16[2048,2048]{1,0:T(8,128)(2,1)} %all-gather.13.cloned.1.call-done, bf16[2048,704]{0,1:T(8,128)(2,1)} %copy-done.63, bf16[2048,704]{0,1:T(8,128)(2,1)} %copy-done.62), kind=kOutput, calls=%fused_computation.4 | convolution fusion | flops 11825577984 | bytes 19922944 | tf_op jit(solution)/shard_map/dot_general | solution.py:64
  792.6 8.3 copy.243
  800.9 5.6 all-to-all-start.5
  806.8 11.0 %convolution_bitcast_fusion = f32[1,704,2048]{2,1,0:T(8,128)} fusion(bf16[2048,704]{0,1:T(8,128)(2,1)} %copy-done.22, bf16[2048,2048]{1,0:T(8,128)(2,1)} %all-gather.15.cloned.1.call-done), kind=kOutput, calls=%fused_computation.26 | convolution fusion | flops 5905580032 | bytes 17039360 | tf_op jit(solution)/shard_map/dot_general | solution.py:64
  817.8 67.3 %all-to-all-done.5 = bf16[8,256,1408]{1,2,0:T(8,128)(2,1)} async-done(((bf16[8,256,1408]{1,2,0:T(8,128)(2,1)}), bf16[8,256,1408]{1,2,0:T(8,128)(2,1)}, u32[]{:S(2)}, u32[]{:S(2)}) %all-to-all-start.5) | async-done | bytes 5767200 | tf_op jit(solution)/shard_map/all_to_all | solution.py:99
  885.1 8.3 convert_bitcast_fusion
  893.4 10.1 %copy.244 = f32[256,2,8,704]{0,3,2,1:T(8,128)} copy(f32[256,2,8,704]{0,3,1,2:T(8,128)} %convert_bitcast_fusion) | data formatting | bytes 23068672 | tf_op jit(solution)/shard_map/convert_element_type | solution.py:101
  903.5 12.0 %copy.246 = f32[1,256,11264]{2,1,0:T(8,128)} copy(f32[1,256,11264]{1,2,0:T(8,128)} %bitcast.118) | data formatting | bytes 23068672
  915.4 2.8 fusion.3
  918.3 43.9 %psum.7 = f32[6,2048]{1,0:T(8,128)S(1)} all-reduce(f32[6,2048]{1,0:T(8,128)S(1)} %pad_maximum_fusion.14), channel_id=1, replica_groups=mesh['dp'=8,'expert'=4] {'dp','expert'}, use_global_device_ids=true, to_apply=%region_24.25 | all-reduce | flops 12288 | bytes 98304 | tf_op jit(solution)/shard_map/psum | solution.py:322
  963.6 1.8 convert_element_type.238
  965.3 1.4 fusion.26
  966.8 4.4 fusion.30
  971.2 2.6 copy.245
  (222 shorter events, 36.1 us)
Async XLA Ops:
  7.2 348.5 %copy-start = (bf16[1,704,2048]{2,1,0:T(8,128)(2,1)S(1)}, bf16[1,704,2048]{2,1,0:T(8,128)(2,1)}, u32[]{:S(2)}) copy-start(bf16[1,704,2048]{2,1,0:T(8,128)(2,1)} %param.19) | copy-start | bytes 8650756
  7.2 47.9 %all-gather.7.cloned.1.call-start = ((), (), s32[]{:S(2)}) async-start(), calls=%async_computation.12 | async-start | bytes 2621440 | tf_op jit(solution)/shard_map/all_gather | solution.py:175
  7.9 96.6 %all-gather.9.cloned.1.call-start = ((), (), s32[]{:S(2)}) async-start(), calls=%async_computation.13 | async-start | bytes 7077888 | tf_op jit(solution)/shard_map/all_gather | solution.py:178
  10.4 124.3 %all-gather.11.cloned.1.call-start = ((), (), s32[]{:S(2)}) async-start(), calls=%async_computation.14 | async-start | bytes 2359296 | tf_op jit(solution)/shard_map/all_gather | solution.py:179
  11.1 169.8 %reduce-scatter.7.cloned.1.call-start = ((), (), s32[]{:S(2)}) async-start(), calls=%async_computation.15 | async-start | bytes 2621440 | tf_op jit(solution)/shard_map/reduce_scatter | solution.py:217
  22.9 88.1 %copy-start.29 = (bf16[2048,6]{0,1:T(8,128)(2,1)}, bf16[2048,6]{0,1:T(8,128)(2,1)S(1)}, u32[]{:S(2)}) copy-start(bf16[2048,6]{0,1:T(8,128)(2,1)S(1)} %all_gather.22) | copy-start | bytes 73732
  22.9 88.0 %copy-start.35 = (f32[2048,1]{0,1:T(1,128)}, f32[2048,1]{0,1:T(1,128)S(1)}, u32[]{:S(2)}) copy-start(f32[2048,1]{0,1:T(1,128)S(1)} %get-tuple-element.99) | copy-start | bytes 24580
  22.9 159.3 %copy-start.31 = (f32[2048,1]{0,1:T(1,128)}, f32[2048,1]{0,1:T(1,128)S(1)}, u32[]{:S(2)}) copy-start(f32[2048,1]{0,1:T(1,128)S(1)} %get-tuple-element.98) | copy-start | bytes 24580
  57.2 53.8 %copy-start.44 = (f32[512]{0:T(512)}, f32[512]{0:T(512)S(1)}, u32[]{:S(2)}) copy-start(f32[512]{0:T(512)S(1)} %add_rsqrt_fusion) | copy-start | bytes 6148
  124.5 3.3 copy-start.27
  127.8 2.1 copy-start.14
  127.8 3.5 copy-start.25
  129.2 2.1 copy-start.2
  129.2 2.1 copy-start.33
  133.0 6.9 copy-start.60
  133.0 7.2 copy-start.39
  134.7 46.2 %copy-start.5 = (bf16[128,2048]{1,0:T(8,128)(2,1)S(1)}, bf16[128,2048]{1,0:T(8,128)(2,1)}, u32[]{:S(2)}) copy-start(bf16[128,2048]{1,0:T(8,128)(2,1)} %param.12) | copy-start | bytes 1572868
  139.1 190.8 %all-gather.13.cloned.1.call-start = ((), (), s32[]{:S(2)}) async-start(), calls=%async_computation.16 | async-start | bytes 9437184 | tf_op jit(solution)/shard_map/all_gather | solution.py:124
  141.0 39.9 %copy-start.48 = (pred[128,2]{0,1:T(4,128)(4,1)}, pred[128,2]{0,1:T(4,128)(4,1)S(1)}, u32[]{:S(2)}) copy-start(pred[128,2]{0,1:T(4,128)(4,1)S(1)} %copy.223) | copy-start | bytes 772
  182.2 41.1 %copy-start.46 = (f32[128]{0:T(128)}, f32[128]{0:T(128)S(1)}, u32[]{:S(2)}) copy-start(f32[128]{0:T(128)S(1)} %add_rsqrt_fusion.2) | copy-start | bytes 1540
  214.7 221.4 %reduce-scatter.9.cloned.1.call-start = ((), (), s32[]{:S(2)}) async-start(), calls=%async_computation.17 | async-start | bytes 9437184 | tf_op jit(solution)/shard_map/reduce_scatter | solution.py:127
  436.1 27.6 %all-to-all-start.2 = ((bf16[4,64,2048]{2,1,0:T(8,128)(2,1)}), bf16[4,64,2048]{2,1,0:T(8,128)(2,1)}, u32[]{:S(2)}, u32[]{:S(2)}) async-start(bf16[4,64,2048]{2,1,0:T(8,128)(2,1)} %bitcast.138), calls=%async_computation.4 | async-start | bytes 2097152 | tf_op jit(solution)/shard_map/all_to_all | solution.py:81
  441.2 114.1 %all-gather.15.cloned.1.call-start = ((), (), s32[]{:S(2)}) async-start(), calls=%async_computation.18 | async-start | bytes 9437184 | tf_op jit(solution)/shard_map/all_gather | solution.py:125
  446.3 23.9 %copy-start.40 = (f32[128]{0:T(128)S(1)}, f32[128]{0:T(128)}, u32[]{:S(2)}) copy-start(f32[128]{0:T(128)} %get-tuple-element.70) | copy-start | bytes 1540
  449.3 19.8 %copy-start.57 = (f32[128]{0:T(128)}, f32[128]{0:T(128)S(1)}, u32[]{:S(2)}) copy-start(f32[128]{0:T(128)S(1)} %get-tuple-element.72) | copy-start | bytes 1540
  463.7 5.4 copy-start.59
  463.7 6.6 copy-start.6
  470.2 31.1 %copy-start.42 = (f32[128,2]{0,1:T(2,128)}, f32[128,2]{0,1:T(2,128)S(1)}, u32[]{:S(2)}) copy-start(f32[128,2]{0,1:T(2,128)S(1)} %get-tuple-element.69) | copy-start | bytes 3076
  470.2 31.1 %copy-start.49 = (f32[128]{0:T(128)}, f32[128]{0:T(128)S(1)}, u32[]{:S(2)}) copy-start(f32[128]{0:T(128)S(1)} %get-tuple-element.100) | copy-start | bytes 1540
  470.2 31.1 %copy-start.51 = (f32[128]{0:T(128)}, f32[128]{0:T(128)S(1)}, u32[]{:S(2)}) copy-start(f32[128]{0:T(128)S(1)} %get-tuple-element.101) | copy-start | bytes 1540
  501.3 158.7 %reduce-scatter.11.cloned.1.call-start = ((), (), s32[]{:S(2)}) async-start(), calls=%async_computation.19 | async-start | bytes 9437184 | tf_op jit(solution)/shard_map/reduce_scatter | solution.py:128
  568.5 2.5 copy-start.63
  588.6 76.7 %copy-start.43 = (f32[128,2]{0,1:T(2,128)S(1)}, f32[128,2]{0,1:T(2,128)}, u32[]{:S(2)}) copy-start(f32[128,2]{0,1:T(2,128)} %copy-done.42) | copy-start | bytes 3076
  588.6 76.7 %copy-start.54 = (f32[128]{0:T(128)S(1)}, f32[128]{0:T(128)}, u32[]{:S(2)}) copy-start(f32[128]{0:T(128)} %copy-done.53) | copy-start | bytes 1540
  588.6 76.7 %copy-start.56 = (f32[128]{0:T(128)S(1)}, f32[128]{0:T(128)}, u32[]{:S(2)}) copy-start(f32[128]{0:T(128)} %copy-done.55) | copy-start | bytes 1540
  588.6 76.7 %copy-start.58 = (f32[128]{0:T(128)S(1)}, f32[128]{0:T(128)}, u32[]{:S(2)}) copy-start(f32[128]{0:T(128)} %get-tuple-element.68) | copy-start | bytes 1540
  588.6 99.3 %copy-start.8 = (bf16[128,2048]{1,0:T(8,128)(2,1)S(1)}, bf16[128,2048]{1,0:T(8,128)(2,1)}, u32[]{:S(2)}) copy-start(bf16[128,2048]{1,0:T(8,128)(2,1)} %reduce-scatter.7.cloned.1.call-done) | copy-start | bytes 1572868
  588.7 99.3 %copy-start.30 = (bf16[2048,6]{0,1:T(8,128)(2,1)S(1)}, bf16[2048,6]{0,1:T(8,128)(2,1)}, u32[]{:S(2)}) copy-start(bf16[2048,6]{0,1:T(8,128)(2,1)} %copy-done.29) | copy-start | bytes 73732
  588.7 99.3 %copy-start.32 = (f32[2048,1]{0,1:T(1,128)S(1)}, f32[2048,1]{0,1:T(1,128)}, u32[]{:S(2)}) copy-start(f32[2048,1]{0,1:T(1,128)} %copy-done.31) | copy-start | bytes 24580
  588.7 99.3 %copy-start.47 = (f32[128]{0:T(128)S(1)}, f32[128]{0:T(128)}, u32[]{:S(2)}) copy-start(f32[128]{0:T(128)} %copy-done.46) | copy-start | bytes 1540
  588.7 100.3 %copy-start.7 = (bf16[128,2048]{1,0:T(8,128)(2,1)S(1)}, bf16[128,2048]{1,0:T(8,128)(2,1)}, u32[]{:S(2)}) copy-start(bf16[128,2048]{1,0:T(8,128)(2,1)} %param.23) | copy-start | bytes 1572868
  588.7 100.3 %copy-start.41 = (f32[128]{0:T(128)S(1)}, f32[128]{0:T(128)}, u32[]{:S(2)}) copy-start(f32[128]{0:T(128)} %get-tuple-element.70) | copy-start | bytes 1540
  660.0 27.6 %all-to-all-start.4 = ((bf16[4,64,2048]{2,1,0:T(8,128)(2,1)}), bf16[4,64,2048]{2,1,0:T(8,128)(2,1)S(1)}, u32[]{:S(2)}, u32[]{:S(2)}) async-start(bf16[4,64,2048]{2,1,0:T(8,128)(2,1)} %bitcast.139), calls=%async_computation.7 | async-start | bytes 2097152 | tf_op jit(solution)/shard_map/all_to_all | solution.py:81
  665.1 70.6 %all-gather.17.cloned.1.call-start = ((), (), s32[]{:S(2)}) async-start(), calls=%async_computation.20 | async-start | bytes 2621440 | tf_op jit(solution)/shard_map/all_gather | solution.py:277
  687.6 2.8 copy-start.34
  687.6 2.8 copy-start.38
  687.6 48.1 %copy-start.61 = (bf16[4,128,512]{2,1,0:T(8,128)(2,1)S(1)}, bf16[4,128,512]{2,1,0:T(8,128)(2,1)}, u32[]{:S(2)}) copy-start(bf16[4,128,512]{2,1,0:T(8,128)(2,1)} %fusion.21) | copy-start | bytes 1572868
  689.0 50.9 %copy-start.10 = (f32[128,2048]{1,0:T(8,128)}, f32[128,2048]{1,0:T(8,128)S(1)}, u32[]{:S(2)}) copy-start(f32[128,2048]{1,0:T(8,128)S(1)} %get-tuple-element.107) | copy-start | bytes 3145732
  690.3 273.3 %reduce-scatter.17.cloned.1.call-start = ((), (), s32[]{:S(2)}) async-start(), calls=%async_computation.23 | async-start | bytes 2359296 | tf_op jit(solution)/shard_map/reduce_scatter | solution.py:280
  740.0 225.4 %reduce-scatter.13.cloned.1.call-start = ((), (), s32[]{:S(2)}) async-start(), calls=%async_computation.21 | async-start | bytes 2621440 | tf_op jit(solution)/shard_map/reduce_scatter | solution.py:305
  740.0 3.7 copy-start.3
  745.6 3.8 copy-start.4
  750.6 2.3 copy-start.23
  750.6 2.3 copy-start.24
  756.7 9.8 copy-start.11
  756.7 9.8 copy-start.28
  756.7 9.8 copy-start.36
  756.7 9.8 copy-start.45
  766.2 205.0 %reduce-scatter.15.cloned.1.call-start = ((), (), s32[]{:S(2)}) async-start(), calls=%async_computation.22 | async-start | bytes 7077888 | tf_op jit(solution)/shard_map/reduce_scatter | solution.py:309
  800.9 5.6 copy-start.13
  800.9 84.2 %all-to-all-start.5 = ((bf16[8,256,1408]{1,2,0:T(8,128)(2,1)}), bf16[8,256,1408]{1,2,0:T(8,128)(2,1)}, u32[]{:S(2)}, u32[]{:S(2)}) async-start(bf16[8,256,1408]{1,2,0:T(8,128)(2,1)} %copy.243), calls=%async_computation.11 | async-start | bytes 11534336 | tf_op jit(solution)/shard_map/all_to_all | solution.py:99
  915.4 51.3 %copy-start.50 = (f32[128]{0:T(128)S(1)}, f32[128]{0:T(128)}, u32[]{:S(2)}) copy-start(f32[128]{0:T(128)} %copy-done.49) | copy-start | bytes 1540
  915.4 51.3 %copy-start.52 = (f32[128]{0:T(128)S(1)}, f32[128]{0:T(128)}, u32[]{:S(2)}) copy-start(f32[128]{0:T(128)} %copy-done.51) | copy-start | bytes 1540
  966.7 7.0 copy-start.1
  (15 other events, 22.7 us)
Sparse Core Ops, SparseCore 0:
  9.6 45.4 all-gather.6
  57.5 46.9 all-gather.8
  106.5 28.1 all-gather.10
  139.2 41.6 reduce-scatter.6
  214.9 108.8 all-gather.12
  364.9 71.1 reduce-scatter.8
  501.4 53.8 all-gather.14
  588.8 71.1 reduce-scatter.10
  690.4 45.2 all-gather.16
  740.1 41.5 reduce-scatter.16
  784.0 41.6 reduce-scatter.12
  829.2 76.9 reduce-scatter.14
where the time goes:
time: 991 us; the launch traced here: 981 us
  waiting for transfers between devices  465 us (47%)
  blocking collectives  208 us (21%)
  matrix products  142 us (14%)
  local copies, waits for them, and re-layouts  89.1 us (9%)
  other arithmetic  43.6 us (4%)
  starting transfers between devices  17.2 us (2%)
  between operations  16.3 us (2%)
    all_to_all x1, blocking collectives, by_hidden(): got = lax.all_to_all(pieces, 'dp', split_axis=0, concat_axis=0, tiled=True)  94.9 us
    reduce_scatter x1, waiting for transfers between devices, experts_split_hidden(): out = lax.psum_scatter(out, 'dp', scatter_dimension=0, tiled=True)  71.4 us
    reduce_scatter x1, waiting for transfers between devices, experts_split_hidden(): d_rows = lax.psum_scatter(d_rows, 'dp', scatter_dimension=0, tiled=True)  71.3 us
    all_to_all x1, waiting for transfers between devices, by_rows(): got = lax.all_to_all(pieces, 'dp', split_axis=0, concat_axis=0, tiled=True)  67.3 us
    all_to_all x2, blocking collectives, exchange_experts(): lax.all_to_all(blocks, 'expert', split_axis=0, concat_axis=0, tiled=True)  59.9 us
    all_gather x1, waiting for transfers between devices, experts_split_hidden(): all_d_out = lax.all_gather(d_rows_out, 'dp', axis=0, tiled=True)  54 us
    all_gather x1, waiting for transfers between devices, on_device(): qkv_full = lax.all_gather(w_qkv, 'dp', axis=1, tiled=True)  47.4 us
    all_gather x1, waiting for transfers between devices, on_device(): whole_grad = lax.all_gather(d_attn, 'expert', axis=0, tiled=True)  45.3 us
  transfers between devices with their start and end apart: 15, of which 11 were waited for; matrix products, arithmetic and copies ran while one was open for 18% of the time, Pallas kernels for 0%

commit v1 on v0

--- a/solution.py
+++ b/solution.py
@@ -319,7 +319,12 @@
     small_part = jnp.concatenate(
         [first_gain_part[None], gain_two_part[None], router_part.T], axis=0
     )
-    small_sum = lax.psum(small_part, ("dp", "expert"))
+
+    def work_page(payload, device_axis, peer_axis="dp"):
+        val = lax.psum(lax.psum(payload, axis_name=device_axis), axis_name=peer_axis)
+        return val
+
+    small_sum = work_page(small_part, "expert")
     own_rows = width // dp_size
     small_own = lax.dynamic_slice_in_dim(
         small_sum, lax.axis_index("dp") * own_rows, own_rows, axis=1

time: 991 us -> 992 us (level)
    psum x1 -> x2, blocking collectives: 43.9 us -> 39.8 us  [the longest x1 22.6 us: work_page(): lax.psum(lax.psum(payload, axis_name=device_axis), axis_name=peer_axis)]
where the time goes in v1:
time: 992 us; the launch traced here: 977 us
  waiting for transfers between devices  465 us (47%)
  blocking collectives  204 us (21%)
  matrix products  142 us (14%)
  local copies, waits for them, and re-layouts  89.1 us (9%)
  other arithmetic  43.7 us (4%)
  starting transfers between devices  17.2 us (2%)
  between operations  16.3 us (2%)
    all_to_all x1, blocking collectives, by_hidden(): got = lax.all_to_all(pieces, 'dp', split_axis=0, concat_axis=0, tiled=True)  94.9 us
    reduce_scatter x1, waiting for transfers between devices, experts_split_hidden(): out = lax.psum_scatter(out, 'dp', scatter_dimension=0, tiled=True)  71.3 us
    reduce_scatter x1, waiting for transfers between devices, experts_split_hidden(): d_rows = lax.psum_scatter(d_rows, 'dp', scatter_dimension=0, tiled=True)  71.3 us
    all_to_all x1, waiting for transfers between devices, by_rows(): got = lax.all_to_all(pieces, 'dp', split_axis=0, concat_axis=0, tiled=True)  67.3 us
    all_to_all x2, blocking collectives, exchange_experts(): lax.all_to_all(blocks, 'expert', split_axis=0, concat_axis=0, tiled=True)  59.9 us
    all_gather x1, waiting for transfers between devices, experts_split_hidden(): all_d_out = lax.all_gather(d_rows_out, 'dp', axis=0, tiled=True)  54 us
    all_gather x1, waiting for transfers between devices, on_device(): qkv_full = lax.all_gather(w_qkv, 'dp', axis=1, tiled=True)  47.4 us
    all_gather x1, waiting for transfers between devices, on_device(): whole_grad = lax.all_gather(d_attn, 'expert', axis=0, tiled=True)  45.3 us
  transfers between devices with their start and end apart: 15, of which 11 were waited for; matrix products, arithmetic and copies ran while one was open for 18% of the time, Pallas kernels for 0%

profile of v1, /device:TPU:10, one launch (start us, length us, event | category | flops | bytes accessed | tf_op | source)
XLA Modules:
  0.0 976.8 jit_solution(420965412824298991)
XLA Ops:
  8.0 2.4 copy.213
  13.8 9.1 all_gather.22
  23.8 1.7 fusion.41
  25.5 29.6 %all-gather.7.cloned.1.call-done = bf16[512,2048]{1,0:T(8,128)(2,1)} async-done(((bf16[128,2048]{1,0:T(8,128)(2,1)}), bf16[512,2048]{1,0:T(8,128)(2,1)}) %all-gather.7.cloned.1.call-update) | async-done | bytes 2097168 | tf_op jit(solution)/shard_map/all_gather | solution.py:175
  55.1 2.1 fusion.4
  57.2 47.4 %all-gather.9.cloned.1.call-done = bf16[3,2048,512]{1,2,0:T(8,128)(2,1)} async-done(((bf16[3,256,512]{1,2,0:T(8,128)(2,1)}), bf16[3,2048,512]{1,2,0:T(8,128)(2,1)}) %all-gather.9.cloned.1.call-update) | async-done | bytes 6291472 | tf_op jit(solution)/shard_map/all_gather | solution.py:178
  104.6 6.4 convolution_bitcast_fusion.1
  113.9 2.4 copy.260
  116.2 2.2 fusion.66
  118.5 2.4 copy.262
  120.8 1.3 copy.259
  122.1 2.4 copy.261
  124.5 3.3 subtract_convert_fusion.3
  127.8 1.4 fusion.68
  129.9 1.4 copy-done.2
  131.3 1.7 fusion.21
  133.0 1.7 all-gather.11.cloned.1.call-done
  134.7 4.4 convolution_convert_fusion.4
  141.3 39.5 %reduce-scatter.7.cloned.1.call-done = bf16[128,2048]{1,0:T(8,128)(2,1)} async-done(((bf16[512,2048]{1,0:T(8,128)(2,1)}), bf16[128,2048]{1,0:T(8,128)(2,1)}) %reduce-scatter.7.cloned.1.call-update) | async-done | bytes 524304 | tf_op jit(solution)/shard_map/reduce_scatter | solution.py:217
  184.7 30.0 %all_to_all.30 = bf16[4,64,2048]{2,1,0:T(8,128)(2,1)} all-to-all(bf16[4,64,2048]{2,1,0:T(8,128)(2,1)S(1)} %bitcast.127), channel_id=1, replica_groups=mesh['dp'=8,'expert'=4] {'expert'}, dimensions={0} | all-to-all | bytes 2097152 | tf_op jit(solution)/shard_map/all_to_all | solution.py:81
  214.9 8.4 copy.224
  223.3 3.4 copy.225
  226.8 94.9 %all_to_all.31 = bf16[8,256,1408]{1,2,0:T(8,128)(2,1)} all-to-all(bf16[8,256,1408]{1,2,0:T(8,128)(2,1)S(1)} %bitcast.119), channel_id=1, replica_groups=mesh['dp'=8,'expert'=4] {'dp'}, dimensions={0} | all-to-all | bytes 11534336 | tf_op jit(solution)/shard_map/all_to_all | solution.py:90
  321.6 8.2 copy.226
  329.9 18.8 %fusion.69 = f32[2048,1408]{0,1:T(8,128)} fusion(bf16[2048,2048]{1,0:T(8,128)(2,1)} %all-gather.13.cloned.1.call-done, bf16[2048,1408]{1,0:T(8,128)(2,1)} %bitcast.121), kind=kOutput, calls=%fused_computation.161 | convolution fusion | flops 11811160064 | bytes 25690112 | tf_op jit(solution)/shard_map/dot_general | solution.py:106
  348.7 5.2 multiply_convert_fusion.2
  354.0 1.7 copy-done.22
  355.6 9.1 convolution_convert_fusion.1
  364.7 71.3 %reduce-scatter.9.cloned.1.call-done = bf16[256,2048]{1,0:T(8,128)(2,1)} async-done(((bf16[2048,2048]{1,0:T(8,128)(2,1)}), bf16[256,2048]{1,0:T(8,128)(2,1)}) %reduce-scatter.9.cloned.1.call-update) | async-done | bytes 1048592 | tf_op jit(solution)/shard_map/reduce_scatter | solution.py:127
  436.1 5.1 all-to-all-start.2
  443.9 2.4 gather_fusion
  447.1 1.5 copy.220
  449.8 13.9 %all-to-all-done.2 = bf16[4,64,2048]{2,1,0:T(8,128)(2,1)} async-done(((bf16[4,64,2048]{2,1,0:T(8,128)(2,1)}), bf16[4,64,2048]{2,1,0:T(8,128)(2,1)}, u32[]{:S(2)}, u32[]{:S(2)}) %all-to-all-start.2) | async-done | bytes 1048608 | tf_op jit(solution)/shard_map/all_to_all | solution.py:81
  463.7 1.6 fusion.44
  466.3 2.8 multiply_reduce_fusion.4
  471.4 29.9 %all_to_all.32 = bf16[4,64,2048]{2,1,0:T(8,128)(2,1)} all-to-all(bf16[4,64,2048]{2,1,0:T(8,128)(2,1)S(1)} %bitcast.130), channel_id=1, replica_groups=mesh['dp'=8,'expert'=4] {'expert'}, dimensions={0} | all-to-all | bytes 2097152 | tf_op jit(solution)/shard_map/all_to_all | solution.py:81
  501.4 54.0 %all-gather.15.cloned.1.call-done = bf16[2048,2048]{1,0:T(8,128)(2,1)} async-done(((bf16[256,2048]{1,0:T(8,128)(2,1)}), bf16[2048,2048]{1,0:T(8,128)(2,1)}) %all-gather.15.cloned.1.call-update) | async-done | bytes 8388624 | tf_op jit(solution)/shard_map/all_gather | solution.py:125
  555.4 13.1 %multiply_convert_fusion.1 = (bf16[2048,704]{0,1:T(8,128)(2,1)S(1)}, bf16[2048,704]{0,1:T(8,128)(2,1)S(1)}) fusion(f32[2048,1408]{0,1:T(8,128)} %fusion.69, bf16[2048,2048]{1,0:T(8,128)(2,1)} %all-gather.15.cloned.1.call-done, bf16[1,704,2048]{2,1,0:T(8,128)(2,1)S(1)} %copy-done), kind=kOutput, calls=%fused_computation.8 | convolution fusion | flops 5924323328 | bytes 28573696 | tf_op jit(solution)/shard_map/dot_general | solution.py:70
  568.5 1.5 copy-done.62
  570.9 17.7 %convolution_convert_fusion = bf16[2048,2048]{1,0:T(8,128)(2,1)} fusion(bf16[2048,1408]{1,0:T(8,128)(2,1)} %bitcast.122, bf16[2048,704]{0,1:T(8,128)(2,1)S(1)} %get-tuple-element.75, bf16[2048,704]{0,1:T(8,128)(2,1)S(1)} %get-tuple-element.74), kind=kOutput, calls=%fused_computation.2 | convolution fusion | flops 11826888704 | bytes 19922944 | tf_op jit(solution)/shard_map/dot_general | solution.py:70
  588.7 71.3 %reduce-scatter.11.cloned.1.call-done = bf16[256,2048]{1,0:T(8,128)(2,1)} async-done(((bf16[2048,2048]{1,0:T(8,128)(2,1)}), bf16[256,2048]{1,0:T(8,128)(2,1)}) %reduce-scatter.11.cloned.1.call-update) | async-done | bytes 1048592 | tf_op jit(solution)/shard_map/reduce_scatter | solution.py:128
  660.0 5.1 all-to-all-start.4
  665.3 22.2 %all-to-all-done.4 = bf16[4,64,2048]{2,1,0:T(8,128)(2,1)S(1)} async-done(((bf16[4,64,2048]{2,1,0:T(8,128)(2,1)}), bf16[4,64,2048]{2,1,0:T(8,128)(2,1)S(1)}, u32[]{:S(2)}, u32[]{:S(2)}) %all-to-all-start.4) | async-done | bytes 1048608 | tf_op jit(solution)/shard_map/all_to_all | solution.py:81
  690.3 45.3 %all-gather.17.cloned.1.call-done = bf16[512,2048]{1,0:T(8,128)(2,1)} async-done(((bf16[128,2048]{1,0:T(8,128)(2,1)}), bf16[512,2048]{1,0:T(8,128)(2,1)}) %all-gather.17.cloned.1.call-update) | async-done | bytes 2097168 | tf_op jit(solution)/shard_map/all_gather | solution.py:277
  735.7 4.2 convolution_convert_fusion.3
  740.0 3.7 convolution_convert_fusion.6
  745.5 3.4 multiply_reduce_fusion
  756.7 9.5 bitcast_convert_fusion
  766.5 6.9 convert_bitcast_fusion.1
  773.4 19.1 %convolution_convert_fusion.2 = bf16[2048,1408]{1,0:T(8,128)(2,1)} fusion(bf16[2048,2048]{1,0:T(8,128)(2,1)} %all-gather.13.cloned.1.call-done, bf16[2048,704]{0,1:T(8,128)(2,1)} %copy-done.63, bf16[2048,704]{0,1:T(8,128)(2,1)} %copy-done.62), kind=kOutput, calls=%fused_computation.4 | convolution fusion | flops 11825577984 | bytes 19922944 | tf_op jit(solution)/shard_map/dot_general | solution.py:64
  792.5 8.3 copy.243
  800.8 5.6 all-to-all-start.5
  806.7 11.0 %convolution_bitcast_fusion = f32[1,704,2048]{2,1,0:T(8,128)} fusion(bf16[2048,704]{0,1:T(8,128)(2,1)} %copy-done.22, bf16[2048,2048]{1,0:T(8,128)(2,1)} %all-gather.15.cloned.1.call-done), kind=kOutput, calls=%fused_computation.26 | convolution fusion | flops 5905580032 | bytes 17039360 | tf_op jit(solution)/shard_map/dot_general | solution.py:64
  817.7 67.3 %all-to-all-done.5 = bf16[8,256,1408]{1,2,0:T(8,128)(2,1)} async-done(((bf16[8,256,1408]{1,2,0:T(8,128)(2,1)}), bf16[8,256,1408]{1,2,0:T(8,128)(2,1)}, u32[]{:S(2)}, u32[]{:S(2)}) %all-to-all-start.5) | async-done | bytes 5767200 | tf_op jit(solution)/shard_map/all_to_all | solution.py:99
  885.0 8.3 convert_bitcast_fusion
  893.4 10.1 %copy.244 = f32[256,2,8,704]{0,3,2,1:T(8,128)} copy(f32[256,2,8,704]{0,3,1,2:T(8,128)} %convert_bitcast_fusion) | data formatting | bytes 23068672 | tf_op jit(solution)/shard_map/convert_element_type | solution.py:101
  903.4 12.0 %copy.246 = f32[1,256,11264]{2,1,0:T(8,128)} copy(f32[1,256,11264]{1,2,0:T(8,128)} %bitcast.118) | data formatting | bytes 23068672
  915.4 2.8 fusion.3
  918.3 17.2 %psum.14 = f32[6,2048]{1,0:T(8,128)S(1)} all-reduce(f32[6,2048]{1,0:T(8,128)S(1)} %pad_maximum_fusion.14), channel_id=1, replica_groups=mesh['dp'=8,'expert'=4] {'expert'}, use_global_device_ids=true, to_apply=%region_24.25 | all-reduce | flops 12288 | bytes 98304 | tf_op jit(solution)/shard_map/psum | solution.py:324
  935.5 22.6 %psum.15 = f32[6,2048]{1,0:T(8,128)S(1)} all-reduce(f32[6,2048]{1,0:T(8,128)S(1)} %psum.14), channel_id=1, replica_groups=mesh['dp'=8,'expert'=4] {'dp'}, use_global_device_ids=true, to_apply=%region_25.26 | all-reduce | flops 12288 | bytes 98304 | tf_op jit(solution)/shard_map/psum | solution.py:324
  959.3 1.8 convert_element_type.238
  961.1 1.4 fusion.26
  962.5 4.4 fusion.30
  967.0 2.6 copy.245
  (223 shorter events, 37.4 us)
Async XLA Ops:
  7.2 348.5 %copy-start = (bf16[1,704,2048]{2,1,0:T(8,128)(2,1)S(1)}, bf16[1,704,2048]{2,1,0:T(8,128)(2,1)}, u32[]{:S(2)}) copy-start(bf16[1,704,2048]{2,1,0:T(8,128)(2,1)} %param.19) | copy-start | bytes 8650756
  7.2 47.9 %all-gather.7.cloned.1.call-start = ((), (), s32[]{:S(2)}) async-start(), calls=%async_computation.12 | async-start | bytes 2621440 | tf_op jit(solution)/shard_map/all_gather | solution.py:175
  7.9 96.6 %all-gather.9.cloned.1.call-start = ((), (), s32[]{:S(2)}) async-start(), calls=%async_computation.13 | async-start | bytes 7077888 | tf_op jit(solution)/shard_map/all_gather | solution.py:178
  10.4 124.3 %all-gather.11.cloned.1.call-start = ((), (), s32[]{:S(2)}) async-start(), calls=%async_computation.14 | async-start | bytes 2359296 | tf_op jit(solution)/shard_map/all_gather | solution.py:179
  11.1 169.8 %reduce-scatter.7.cloned.1.call-start = ((), (), s32[]{:S(2)}) async-start(), calls=%async_computation.15 | async-start | bytes 2621440 | tf_op jit(solution)/shard_map/reduce_scatter | solution.py:217
  22.9 88.1 %copy-start.29 = (bf16[2048,6]{0,1:T(8,128)(2,1)}, bf16[2048,6]{0,1:T(8,128)(2,1)S(1)}, u32[]{:S(2)}) copy-start(bf16[2048,6]{0,1:T(8,128)(2,1)S(1)} %all_gather.22) | copy-start | bytes 73732
  22.9 88.0 %copy-start.35 = (f32[2048,1]{0,1:T(1,128)}, f32[2048,1]{0,1:T(1,128)S(1)}, u32[]{:S(2)}) copy-start(f32[2048,1]{0,1:T(1,128)S(1)} %get-tuple-element.99) | copy-start | bytes 24580
  22.9 159.3 %copy-start.31 = (f32[2048,1]{0,1:T(1,128)}, f32[2048,1]{0,1:T(1,128)S(1)}, u32[]{:S(2)}) copy-start(f32[2048,1]{0,1:T(1,128)S(1)} %get-tuple-element.98) | copy-start | bytes 24580
  57.2 53.8 %copy-start.44 = (f32[512]{0:T(512)}, f32[512]{0:T(512)S(1)}, u32[]{:S(2)}) copy-start(f32[512]{0:T(512)S(1)} %add_rsqrt_fusion) | copy-start | bytes 6148
  124.5 3.3 copy-start.27
  127.8 2.0 copy-start.14
  127.8 3.4 copy-start.25
  129.2 2.1 copy-start.2
  129.2 2.0 copy-start.33
  133.0 7.0 copy-start.60
  133.0 7.2 copy-start.39
  134.7 46.2 %copy-start.5 = (bf16[128,2048]{1,0:T(8,128)(2,1)S(1)}, bf16[128,2048]{1,0:T(8,128)(2,1)}, u32[]{:S(2)}) copy-start(bf16[128,2048]{1,0:T(8,128)(2,1)} %param.12) | copy-start | bytes 1572868
  139.1 190.7 %all-gather.13.cloned.1.call-start = ((), (), s32[]{:S(2)}) async-start(), calls=%async_computation.16 | async-start | bytes 9437184 | tf_op jit(solution)/shard_map/all_gather | solution.py:124
  141.0 39.8 %copy-start.48 = (pred[128,2]{0,1:T(4,128)(4,1)}, pred[128,2]{0,1:T(4,128)(4,1)S(1)}, u32[]{:S(2)}) copy-start(pred[128,2]{0,1:T(4,128)(4,1)S(1)} %copy.223) | copy-start | bytes 772
  182.2 41.2 %copy-start.46 = (f32[128]{0:T(128)}, f32[128]{0:T(128)S(1)}, u32[]{:S(2)}) copy-start(f32[128]{0:T(128)S(1)} %add_rsqrt_fusion.2) | copy-start | bytes 1540
  214.7 221.4 %reduce-scatter.9.cloned.1.call-start = ((), (), s32[]{:S(2)}) async-start(), calls=%async_computation.17 | async-start | bytes 9437184 | tf_op jit(solution)/shard_map/reduce_scatter | solution.py:127
  436.1 27.6 %all-to-all-start.2 = ((bf16[4,64,2048]{2,1,0:T(8,128)(2,1)}), bf16[4,64,2048]{2,1,0:T(8,128)(2,1)}, u32[]{:S(2)}, u32[]{:S(2)}) async-start(bf16[4,64,2048]{2,1,0:T(8,128)(2,1)} %bitcast.138), calls=%async_computation.4 | async-start | bytes 2097152 | tf_op jit(solution)/shard_map/all_to_all | solution.py:81
  441.2 114.2 %all-gather.15.cloned.1.call-start = ((), (), s32[]{:S(2)}) async-start(), calls=%async_computation.18 | async-start | bytes 9437184 | tf_op jit(solution)/shard_map/all_gather | solution.py:125
  446.3 23.9 %copy-start.40 = (f32[128]{0:T(128)S(1)}, f32[128]{0:T(128)}, u32[]{:S(2)}) copy-start(f32[128]{0:T(128)} %get-tuple-element.70) | copy-start | bytes 1540
  449.2 19.8 %copy-start.57 = (f32[128]{0:T(128)}, f32[128]{0:T(128)S(1)}, u32[]{:S(2)}) copy-start(f32[128]{0:T(128)S(1)} %get-tuple-element.72) | copy-start | bytes 1540
  463.7 5.4 copy-start.59
  463.7 6.6 copy-start.6
  470.2 31.1 %copy-start.42 = (f32[128,2]{0,1:T(2,128)}, f32[128,2]{0,1:T(2,128)S(1)}, u32[]{:S(2)}) copy-start(f32[128,2]{0,1:T(2,128)S(1)} %get-tuple-element.69) | copy-start | bytes 3076
  470.2 31.1 %copy-start.49 = (f32[128]{0:T(128)}, f32[128]{0:T(128)S(1)}, u32[]{:S(2)}) copy-start(f32[128]{0:T(128)S(1)} %get-tuple-element.100) | copy-start | bytes 1540
  470.2 31.1 %copy-start.51 = (f32[128]{0:T(128)}, f32[128]{0:T(128)S(1)}, u32[]{:S(2)}) copy-start(f32[128]{0:T(128)S(1)} %get-tuple-element.101) | copy-start | bytes 1540
  501.3 158.6 %reduce-scatter.11.cloned.1.call-start = ((), (), s32[]{:S(2)}) async-start(), calls=%async_computation.19 | async-start | bytes 9437184 | tf_op jit(solution)/shard_map/reduce_scatter | solution.py:128
  568.5 2.4 copy-start.63
  588.6 76.7 %copy-start.43 = (f32[128,2]{0,1:T(2,128)S(1)}, f32[128,2]{0,1:T(2,128)}, u32[]{:S(2)}) copy-start(f32[128,2]{0,1:T(2,128)} %copy-done.42) | copy-start | bytes 3076
  588.6 76.7 %copy-start.54 = (f32[128]{0:T(128)S(1)}, f32[128]{0:T(128)}, u32[]{:S(2)}) copy-start(f32[128]{0:T(128)} %copy-done.53) | copy-start | bytes 1540
  588.6 76.7 %copy-start.56 = (f32[128]{0:T(128)S(1)}, f32[128]{0:T(128)}, u32[]{:S(2)}) copy-start(f32[128]{0:T(128)} %copy-done.55) | copy-start | bytes 1540
  588.6 76.7 %copy-start.58 = (f32[128]{0:T(128)S(1)}, f32[128]{0:T(128)}, u32[]{:S(2)}) copy-start(f32[128]{0:T(128)} %get-tuple-element.68) | copy-start | bytes 1540
  588.6 99.3 %copy-start.8 = (bf16[128,2048]{1,0:T(8,128)(2,1)S(1)}, bf16[128,2048]{1,0:T(8,128)(2,1)}, u32[]{:S(2)}) copy-start(bf16[128,2048]{1,0:T(8,128)(2,1)} %reduce-scatter.7.cloned.1.call-done) | copy-start | bytes 1572868
  588.6 99.3 %copy-start.30 = (bf16[2048,6]{0,1:T(8,128)(2,1)S(1)}, bf16[2048,6]{0,1:T(8,128)(2,1)}, u32[]{:S(2)}) copy-start(bf16[2048,6]{0,1:T(8,128)(2,1)} %copy-done.29) | copy-start | bytes 73732
  588.7 99.3 %copy-start.32 = (f32[2048,1]{0,1:T(1,128)S(1)}, f32[2048,1]{0,1:T(1,128)}, u32[]{:S(2)}) copy-start(f32[2048,1]{0,1:T(1,128)} %copy-done.31) | copy-start | bytes 24580
  588.7 99.3 %copy-start.47 = (f32[128]{0:T(128)S(1)}, f32[128]{0:T(128)}, u32[]{:S(2)}) copy-start(f32[128]{0:T(128)} %copy-done.46) | copy-start | bytes 1540
  588.7 100.3 %copy-start.7 = (bf16[128,2048]{1,0:T(8,128)(2,1)S(1)}, bf16[128,2048]{1,0:T(8,128)(2,1)}, u32[]{:S(2)}) copy-start(bf16[128,2048]{1,0:T(8,128)(2,1)} %param.23) | copy-start | bytes 1572868
  588.7 100.3 %copy-start.41 = (f32[128]{0:T(128)S(1)}, f32[128]{0:T(128)}, u32[]{:S(2)}) copy-start(f32[128]{0:T(128)} %get-tuple-element.70) | copy-start | bytes 1540
  660.0 27.6 %all-to-all-start.4 = ((bf16[4,64,2048]{2,1,0:T(8,128)(2,1)}), bf16[4,64,2048]{2,1,0:T(8,128)(2,1)S(1)}, u32[]{:S(2)}, u32[]{:S(2)}) async-start(bf16[4,64,2048]{2,1,0:T(8,128)(2,1)} %bitcast.139), calls=%async_computation.7 | async-start | bytes 2097152 | tf_op jit(solution)/shard_map/all_to_all | solution.py:81
  665.1 70.6 %all-gather.17.cloned.1.call-start = ((), (), s32[]{:S(2)}) async-start(), calls=%async_computation.20 | async-start | bytes 2621440 | tf_op jit(solution)/shard_map/all_gather | solution.py:277
  687.5 2.8 copy-start.34
  687.6 2.8 copy-start.38
  687.6 48.1 %copy-start.61 = (bf16[4,128,512]{2,1,0:T(8,128)(2,1)S(1)}, bf16[4,128,512]{2,1,0:T(8,128)(2,1)}, u32[]{:S(2)}) copy-start(bf16[4,128,512]{2,1,0:T(8,128)(2,1)} %fusion.21) | copy-start | bytes 1572868
  689.0 50.9 %copy-start.10 = (f32[128,2048]{1,0:T(8,128)}, f32[128,2048]{1,0:T(8,128)S(1)}, u32[]{:S(2)}) copy-start(f32[128,2048]{1,0:T(8,128)S(1)} %get-tuple-element.107) | copy-start | bytes 3145732
  690.2 269.1 %reduce-scatter.17.cloned.1.call-start = ((), (), s32[]{:S(2)}) async-start(), calls=%async_computation.23 | async-start | bytes 2359296 | tf_op jit(solution)/shard_map/reduce_scatter | solution.py:280
  739.9 221.2 %reduce-scatter.13.cloned.1.call-start = ((), (), s32[]{:S(2)}) async-start(), calls=%async_computation.21 | async-start | bytes 2621440 | tf_op jit(solution)/shard_map/reduce_scatter | solution.py:305
  740.0 3.7 copy-start.3
  745.5 3.8 copy-start.4
  750.6 2.3 copy-start.23
  750.6 2.3 copy-start.24
  756.6 9.8 %copy-start.11 = (bf16[512,2048]{1,0:T(8,128)(2,1)S(1)}, bf16[512,2048]{1,0:T(8,128)(2,1)}, u32[]{:S(2)}) copy-start(bf16[512,2048]{1,0:T(8,128)(2,1)} %all-gather.7.cloned.1.call-done) | copy-start | bytes 6291460
  756.6 9.8 %copy-start.28 = (bf16[1,512,512]{2,1,0:T(8,128)(2,1)S(1)}, bf16[1,512,512]{2,1,0:T(8,128)(2,1)}, u32[]{:S(2)}) copy-start(bf16[1,512,512]{2,1,0:T(8,128)(2,1)} %copy.240) | copy-start | bytes 1572868
  756.6 9.8 %copy-start.36 = (f32[2048,1]{0,1:T(1,128)S(1)}, f32[2048,1]{0,1:T(1,128)}, u32[]{:S(2)}) copy-start(f32[2048,1]{0,1:T(1,128)} %copy-done.35) | copy-start | bytes 24580
  756.7 9.8 %copy-start.45 = (f32[512]{0:T(512)S(1)}, f32[512]{0:T(512)}, u32[]{:S(2)}) copy-start(f32[512]{0:T(512)} %copy-done.44) | copy-start | bytes 6148
  766.2 200.8 %reduce-scatter.15.cloned.1.call-start = ((), (), s32[]{:S(2)}) async-start(), calls=%async_computation.22 | async-start | bytes 7077888 | tf_op jit(solution)/shard_map/reduce_scatter | solution.py:309
  800.8 5.6 copy-start.13
  800.8 84.2 %all-to-all-start.5 = ((bf16[8,256,1408]{1,2,0:T(8,128)(2,1)}), bf16[8,256,1408]{1,2,0:T(8,128)(2,1)}, u32[]{:S(2)}, u32[]{:S(2)}) async-start(bf16[8,256,1408]{1,2,0:T(8,128)(2,1)} %copy.243), calls=%async_computation.11 | async-start | bytes 11534336 | tf_op jit(solution)/shard_map/all_to_all | solution.py:99
  915.4 47.1 %copy-start.50 = (f32[128]{0:T(128)S(1)}, f32[128]{0:T(128)}, u32[]{:S(2)}) copy-start(f32[128]{0:T(128)} %copy-done.49) | copy-start | bytes 1540
  915.4 47.1 %copy-start.52 = (f32[128]{0:T(128)S(1)}, f32[128]{0:T(128)}, u32[]{:S(2)}) copy-start(f32[128]{0:T(128)} %copy-done.51) | copy-start | bytes 1540
  962.5 7.0 copy-start.1
  (15 other events, 22.7 us)
Sparse Core Ops, SparseCore 0:
  9.6 45.4 all-gather.6
  57.5 46.9 all-gather.8
  106.5 28.1 all-gather.10
  139.2 41.5 reduce-scatter.6
  214.8 108.8 all-gather.12
  364.9 71.1 reduce-scatter.8
  501.4 53.8 all-gather.14
  588.8 71.1 reduce-scatter.10
  690.4 45.2 all-gather.16
  740.0 41.4 reduce-scatter.16
  783.9 41.6 reduce-scatter.12
  829.2 76.9 reduce-scatter.14
